TPU v7x, 32 devices: a whole 2x2x4 slice. The times are simulated.
32 devices in a mesh: batch: 8 (over z, x), tok: 4 (over y, core).
Axes of the slice: x: 2, y: 2, z: 4, core: 2. Of those that a mesh axis runs over, the one named last changes fastest.
Arguments:
- patches: bfloat16 [24, 1024, 768], P('batch', 'tok'), may hold values from -6 to 6
- image_ids: int32 [24, 1024], P('batch', 'tok'), may hold values from -1 to 3, as said below
- cotangent: bfloat16 [24, 1024, 768], P('batch', 'tok'), may hold values from -6 to 6
- norm_gain: float32 [768], replicated, may hold values from 0.25 to 1.75
- query_gain: float32 [64], replicated, may hold values from 0.25 to 1.75
- key_gain: float32 [64], replicated, may hold values from 0.25 to 1.75
- in_weight: bfloat16 [768, 5376], P(('batch', 'tok')), may hold values from -0.21875 to 0.21875
- out_weight: bfloat16 [3840, 768], P(('batch', 'tok')), may hold values from -0.6538492 to 0.6538492
Outputs:
- block_out: bfloat16 [24, 1024, 768], P('batch', 'tok')
- patch_grad: bfloat16 [24, 1024, 768], P('batch', 'tok')
- norm_grad: float32 [768], replicated
- query_grad: float32 [64], replicated
- key_grad: float32 [64], replicated
- in_grad: float32 [768, 5376], P(('batch', 'tok'))
- out_grad: float32 [3840, 768], P(('batch', 'tok'))
Inputs may be any that keep to these rules, and one draw needn't show every extreme that they name: `image_ids`: in each sequence the ids of the live tokens run 0, 1, 2, 3 in contiguous non-decreasing runs (a run may be empty; the last image is never empty), followed by at least one padding slot of -1 at the end of the sequence.
All inputs are finite; a program needn't handle non-finite values.
Results may differ from a plain program's by a relative error of at most 0.0097.
Values may be sent and summed in bfloat16 or wider, within the bound.
No kernel may reach another device: no remote copies, remote signals or barrier semaphores. Data moves between devices by JAX's collectives and lax.ppermute only.
A program may use at most 192 MiB of HBM per device.

v0:
```python
import math
import jax
import jax.numpy as jnp
from jax import lax
from jax.sharding import PartitionSpec as P

H = 12
HD = 64
mask_fill = -1000000000.0
norm_eps = 1e-06


def normalize(values):
    center = values - jnp.mean(values, axis=-1, keepdims=True)
    inverse = lax.rsqrt(jnp.mean(center * center, axis=-1, keepdims=True) + norm_eps)
    return (center * inverse, inverse)


def norm_back(grad_unit, unit_rows, inverse):
    return inverse * (
        grad_unit
        - jnp.mean(grad_unit, axis=-1, keepdims=True)
        - unit_rows * jnp.mean(grad_unit * unit_rows, axis=-1, keepdims=True)
    )


def head_scores(query_block, key_block, seq_ids):
    score_scale = 1.0 / math.sqrt(query_block.shape[-1])
    scores = (
        jnp.einsum("qhd,khd->hqk", query_block, key_block, preferred_element_type=jnp.float32)
        * score_scale
    )
    allowed = (seq_ids[:, None] == seq_ids[None, :]) & (seq_ids[:, None] >= 0)
    return jnp.where(allowed[None], scores, mask_fill)


def forward_sequence(inputs):
    query_block, key_block, value_block, seq_ids = inputs
    scores = head_scores(query_block, key_block, seq_ids)
    row_max = jnp.max(scores, axis=-1, keepdims=True)
    weights = jnp.exp(scores - row_max)
    row_total = jnp.sum(weights, axis=-1, keepdims=True)
    probabilities = (weights / row_total).astype(jnp.bfloat16)
    outputs = jnp.einsum(
        "hqk,khd->qhd", probabilities, value_block, preferred_element_type=jnp.float32
    )
    return (outputs.astype(jnp.bfloat16), (row_max + jnp.log(row_total))[..., 0])


def backward_sequence(inputs):
    query_block, key_block, value_block, seq_ids, log_total, grad_out = inputs
    score_scale = 1.0 / math.sqrt(query_block.shape[-1])
    scores = head_scores(query_block, key_block, seq_ids)
    probabilities = jnp.exp(scores - log_total[..., None])
    grad_probs = jnp.einsum(
        "qhd,khd->hqk", grad_out, value_block, preferred_element_type=jnp.float32
    )
    weighted = jnp.sum(probabilities * grad_probs, axis=-1, keepdims=True)
    grad_scores = (probabilities * (grad_probs - weighted)).astype(jnp.bfloat16)
    grad_query = score_scale * jnp.einsum(
        "hqk,khd->qhd", grad_scores, key_block, preferred_element_type=jnp.float32
    )
    grad_key = score_scale * jnp.einsum(
        "hqk,qhd->khd", grad_scores, query_block, preferred_element_type=jnp.float32
    )
    grad_value = jnp.einsum(
        "hqk,qhd->khd",
        probabilities.astype(jnp.bfloat16),
        grad_out,
        preferred_element_type=jnp.float32,
    )
    return (
        grad_query.astype(jnp.bfloat16),
        grad_key.astype(jnp.bfloat16),
        grad_value.astype(jnp.bfloat16),
    )


def per_device(
    patches, image_ids, cotangent, norm_gain, query_gain, key_gain, in_weight, out_weight
):
    seq_count, part_len, feature_width = patches.shape
    row_count = seq_count * part_len
    contract_last = (((1,), (1,)), ((), ()))
    contract_first = (((0,), (0,)), ((), ()))
    live_rows = (image_ids >= 0).astype(jnp.float32).reshape(row_count, 1)
    flat_rows = patches.reshape(row_count, feature_width).astype(jnp.float32)
    unit_rows, inverse = normalize(flat_rows)
    normed = (unit_rows * norm_gain).astype(jnp.bfloat16)
    in_full = lax.all_gather(in_weight, ("batch", "tok"), axis=0, tiled=True)
    merged = jnp.dot(normed, in_full, preferred_element_type=jnp.float32)
    query_unit, query_inverse = normalize(merged[:, :feature_width].reshape(row_count, H, HD))
    key_unit, key_inverse = normalize(
        merged[:, feature_width : 2 * feature_width].reshape(row_count, H, HD)
    )
    head_shape = (seq_count, part_len, H, HD)
    queries = (query_unit * query_gain).astype(jnp.bfloat16).reshape(head_shape)
    key_rows = (key_unit * key_gain).astype(jnp.bfloat16).reshape(head_shape)
    value_rows = (
        merged[:, 2 * feature_width : 3 * feature_width].astype(jnp.bfloat16).reshape(head_shape)
    )
    up_proj = merged[:, 3 * feature_width :]
    hidden = jax.nn.gelu(up_proj).astype(jnp.bfloat16)
    ids_full = lax.all_gather(image_ids, "tok", axis=1, tiled=True)
    query_heads, key_heads, value_heads = (
        lax.all_to_all(queries, "tok", split_axis=2, concat_axis=1, tiled=True),
        lax.all_to_all(key_rows, "tok", split_axis=2, concat_axis=1, tiled=True),
        lax.all_to_all(value_rows, "tok", split_axis=2, concat_axis=1, tiled=True),
    )
    heads_out, log_total = lax.map(
        forward_sequence, (query_heads, key_heads, value_heads, ids_full)
    )
    heads_tok = lax.all_to_all(heads_out, "tok", split_axis=1, concat_axis=2, tiled=True)
    combined = jnp.concatenate([heads_tok.reshape(row_count, feature_width), hidden], axis=1)
    out_full = lax.all_gather(out_weight, ("batch", "tok"), axis=0, tiled=True)
    branch = jnp.dot(combined, out_full, preferred_element_type=jnp.float32)
    block_out = (
        (live_rows * (flat_rows + branch))
        .astype(jnp.bfloat16)
        .reshape(seq_count, part_len, feature_width)
    )
    grad_branch = (
        live_rows * cotangent.reshape(row_count, feature_width).astype(jnp.float32)
    ).astype(jnp.bfloat16)
    out_back = lax.all_gather(out_weight, ("batch", "tok"), axis=0, tiled=True)
    grad_combined = lax.dot_general(
        grad_branch, out_back, contract_last, preferred_element_type=jnp.float32
    )
    grad_heads = grad_combined[:, :feature_width].astype(jnp.bfloat16).reshape(head_shape)
    grad_hidden = grad_combined[:, feature_width:]
    grad_heads_h = lax.all_to_all(grad_heads, "tok", split_axis=2, concat_axis=1, tiled=True)
    grad_query_h, grad_key_h, grad_value_h = lax.map(
        backward_sequence, (query_heads, key_heads, value_heads, ids_full, log_total, grad_heads_h)
    )
    grad_query, grad_key, grad_value = (
        lax.all_to_all(grad_query_h, "tok", split_axis=1, concat_axis=2, tiled=True),
        lax.all_to_all(grad_key_h, "tok", split_axis=1, concat_axis=2, tiled=True),
        lax.all_to_all(grad_value_h, "tok", split_axis=1, concat_axis=2, tiled=True),
    )
    grad_query = grad_query.reshape(row_count, H, HD).astype(jnp.float32)
    grad_key = grad_key.reshape(row_count, H, HD).astype(jnp.float32)
    query_grad = jnp.sum(grad_query * query_unit, axis=(0, 1))
    key_grad = jnp.sum(grad_key * key_unit, axis=(0, 1))
    grad_query_raw = norm_back(grad_query * query_gain, query_unit, query_inverse).reshape(
        row_count, feature_width
    )
    grad_key_raw = norm_back(grad_key * key_gain, key_unit, key_inverse).reshape(
        row_count, feature_width
    )
    unused_value, gelu_pull = jax.vjp(jax.nn.gelu, up_proj)
    grad_up = gelu_pull(grad_hidden)[0]
    grad_merged = jnp.concatenate(
        [
            grad_query_raw,
            grad_key_raw,
            grad_value.reshape(row_count, feature_width).astype(jnp.float32),
            grad_up,
        ],
        axis=1,
    ).astype(jnp.bfloat16)
    in_back = lax.all_gather(in_weight, ("batch", "tok"), axis=0, tiled=True)
    grad_normed = lax.dot_general(
        grad_merged, in_back, contract_last, preferred_element_type=jnp.float32
    )
    columns = combined
    out_grad = lax.psum_scatter(
        lax.dot_general(columns, grad_branch, contract_first, preferred_element_type=jnp.float32),
        ("batch", "tok"),
        scatter_dimension=0,
        tiled=True,
    )
    columns = normed
    in_grad = lax.psum_scatter(
        lax.dot_general(columns, grad_merged, contract_first, preferred_element_type=jnp.float32),
        ("batch", "tok"),
        scatter_dimension=0,
        tiled=True,
    )
    norm_grad = jnp.sum(grad_normed * unit_rows, axis=0)
    norm_grad, query_grad, key_grad = lax.psum((norm_grad, query_grad, key_grad), ("batch", "tok"))
    input_grad = grad_branch.astype(jnp.float32) + norm_back(
        grad_normed * norm_gain, unit_rows, inverse
    )
    patch_grad = input_grad.astype(jnp.bfloat16).reshape(seq_count, part_len, feature_width)
    return (block_out, patch_grad, norm_grad, query_grad, key_grad, in_grad, out_grad)


def solution(mesh):
    return jax.shard_map(
        per_device,
        mesh=mesh,
        in_specs=(
            P("batch", "tok", None),
            P("batch", "tok"),
            P("batch", "tok", None),
            P(),
            P(),
            P(),
            P(("batch", "tok"), None),
            P(("batch", "tok"), None),
        ),
        out_specs=(
            P("batch", "tok", None),
            P("batch", "tok", None),
            P(),
            P(),
            P(),
            P(("batch", "tok"), None),
            P(("batch", "tok"), None),
        ),
        check_vma=False,
    )
```

profile of v0, /device:TPU:0, one launch (start us, length us, event | category | flops | bytes accessed | tf_op | source)
XLA Modules:
  0.0 865.3 jit_solution(12807134748747574468)
XLA Ops:
  13.2 68.2 %all-gather.5.cloned.1.call-done = bf16[3840,768]{1,0:T(8,128)(2,1)} async-done(((bf16[120,768]{1,0:T(8,128)(2,1)}), bf16[3840,768]{1,0:T(8,128)(2,1)}) %all-gather.5.cloned.1.call-update) | async-done | bytes 5898256 | tf_op jit(solution)/shard_map/all_gather | solution.py:115
  104.9 56.8 %all-gather.3.cloned.1.call-done = bf16[768,5376]{1,0:T(8,128)(2,1)} async-done(((bf16[24,5376]{1,0:T(8,128)(2,1)}), bf16[768,5376]{1,0:T(8,128)(2,1)}) %all-gather.3.cloned.1.call-update) | async-done | bytes 8257552 | tf_op jit(solution)/shard_map/all_gather | solution.py:90
  161.7 8.7 %fusion.92 = f32[768,5376]{1,0:T(8,128)S(1)} fusion(bf16[768,768]{1,0:T(8,128)(2,1)S(1)} %copy-done.15, bf16[768,5376]{1,0:T(8,128)(2,1)} %all-gather.3.cloned.1.call-done), kind=kOutput, calls=%fused_computation.141 | convolution fusion | flops 6341787648 | bytes 25952256 | tf_op jit(solution)/shard_map/dot_general | solution.py:91
  191.3 15.2 %all-to-all-start = ((bf16[3,256,12,64]{1,3,0,2:T(8,128)(2,1)}), bf16[3,256,12,64]{1,3,0,2:T(8,128)(2,1)S(1)}, u32[]{:S(2)}, u32[]{:S(2)}) async-start(bf16[3,256,12,64]{1,3,0,2:T(8,128)(2,1)} %copy.166), calls=%async_computation | async-start | bytes 2359296 | tf_op jit(solution)/shard_map/all_to_all | solution.py:108
  245.8 16.8 %all_gather.12 = s32[3,1024]{1,0:T(4,128)S(1)} all-gather(s32[3,256]{1,0:T(4,128)S(1)} %copy-done.32), channel_id=1, replica_groups=mesh['batch'=8,'tok'=4] {'tok'}, dimensions={1}, use_global_device_ids=true | all-gather | bytes 15360 | tf_op jit(solution)/shard_map/all_gather | solution.py:104
  276.7 45.7 %while.26 = (s32[]{:T(128)}, bf16[3,1024,3,64]{1,3,2,0:T(8,128)(2,1)}, f32[3,3,1024]{2,1,0:T(4,128)}, bf16[3,1024,3,64]{1,3,2,0:T(8,128)(2,1)}, s32[3,1024]{1,0:...) while((s32[]{:T(128)}, ...), condition=%wide.region_9.10_spmd, body=%wide.region_6.9_spmd.sunk | while | flops 845346816 | bytes 47833216 | solution.py:110
  334.8 14.1 %fusion.65 = (bf16[768,3072]{1,0:T(8,128)(2,1)}, bf16[768,3072]{1,0:T(8,128)(2,1)}) fusion(f32[768,3840]{1,0:T(8,128)} %copy-done.7, f32[768,5376]{1,0:T(8,128)} %copy-done.1), kind=kLoop, calls=%fused_computation.76 | loop fusion | flops 51904512 | bytes 28311552 | tf_op jit(solution)/shard_map/convert.19
  360.2 11.9 %fusion.66 = f32[3840,768]{1,0:T(8,128)} fusion(bf16[768,768]{1,0:T(8,128)(2,1)S(1)} %copy-done.20, bf16[768,3072]{1,0:T(8,128)(2,1)} %get-tuple-element.157, bf16[768,768]{1,0:T(8,128)(2,1)S(1)} %copy.181), kind=kOutput, calls=%fused_computation.80 | convolution fusion | flops 4541644800 | bytes 18874368 | tf_op jit(solution)/shard_map/dot_general | solution.py:167
  375.8 84.0 %while.27 = (s32[]{:T(128)}, bf16[3,1024,3,64]{1,3,2,0:T(8,128)(2,1)}, bf16[3,1024,3,64]{1,3,2,0:T(8,128)(2,1)}, bf16[3,1024,3,64]{1,3,2,0:T(8,128)(2,1)}, bf16[...) while((s32[]{:T(128)}, ...), condition=%wide.region_12.13_spmd, body=%wide.region_10.12_spmd.sunk | while | flops 2063529984 | bytes 102616192 | solution.py:132
  379.3 8.3 multiply_reduce_fusion.11
  387.6 7.5 multiply_convert_fusion.7
  407.6 8.3 multiply_reduce_fusion.11
  435.4 8.3 multiply_reduce_fusion.11
  479.5 18.2 %all-to-all-done.7 = bf16[4,2,73728]{2,1,0:T(2,128)(2,1)} async-done(((bf16[4,2,73728]{2,1,0:T(2,128)(2,1)}), bf16[4,2,73728]{2,1,0:T(2,128)(2,1)}, u32[]{:S(2)}, u32[]{:S(2)}) %all-to-all-start.7) | async-done | bytes 1179680 | tf_op jit(solution)/shard_map/all_to_all | solution.py:138
  510.0 10.8 %all-to-all-done.5 = bf16[4,2,73728]{2,1,0:T(2,128)(2,1)} async-done(((bf16[4,2,73728]{2,1,0:T(2,128)(2,1)}), bf16[4,2,73728]{2,1,0:T(2,128)(2,1)}, u32[]{:S(2)}, u32[]{:S(2)}) %all-to-all-start.5) | async-done | bytes 1179680 | tf_op jit(solution)/shard_map/all_to_all | solution.py:136
  525.3 7.9 reshape.416
  600.6 8.1 reshape.415
  638.0 7.8 reshape.417
  645.8 9.4 %multiply_convert_fusion.5 = (bf16[768,768]{1,0:T(8,128)(2,1)S(1)}, bf16[768,768]{1,0:T(8,128)(2,1)S(1)}) fusion(f32[768,768]{1,0:T(8,128)S(1)} %copy-done.8, f32[768,768]{1,0:T(8,128)} %copy.199, f32[768,768]{1,0:T(8,128)} %copy.192, f32[768,768]{1,0:T(8,128)} %copy.191, f32[768,768]{1,0:T(8,128)} %reshape.415, f32[768]{0:T(1024)S(1)} %mul.317, ...), kind=kLoop, calls=%fused_computation.113 | loop fusion | flops 9437184 | bytes 30676992 | tf_op jit(solution)/shard_map/convert.16
  656.3 12.3 %fusion.85 = f32[768,5376]{1,0:T(8,128)} fusion(bf16[768,768]{1,0:T(8,128)(2,1)S(1)} %copy-done.16, bf16[768,3072]{1,0:T(8,128)(2,1)} %get-tuple-element.156, bf16[768,768]{1,0:T(8,128)(2,1)S(1)} %copy-done.21, bf16[768,768]{1,0:T(8,128)(2,1)S(1)} %get-tuple-element.155, bf16[768,768]{1,0:T(8,128)(2,1)S(1)} %get-tuple-element.154), kind=kOutput, calls=%fused_computation.121 | convolution fusion | flops 6374817792 | bytes 25952256 | tf_op jit(solution)/shard_map/dot_general | solution.py:174
  669.9 13.3 %fusion.82 = (f32[768]{0:T(1024)}, f32[768]{0:T(1024)}, f32[768]{0:T(1024)}, f32[768,768]{1,0:T(8,128)}) fusion(bf16[3,256,768]{2,1,0:T(8,128)(2,1)S(1)} %copy-done.6, f32[768]{0:T(1024)S(1)} %copy-done.31, f32[768]{0:T(1024)S(1)} %copy-done.29, f32[768]{0:T(1024)S(1)} %copy-done.34, bf16[768,5376]{1,0:T(8,128)(2,1)} %all-gather.3.cloned.1.call-done, ...), kind=kOutput, calls=%fused_computation.105 | convolution fusion | flops 6380123136 | bytes 20072448 | tf_op jit(solution)/shard_map/dot_general | solution.py:162
  683.2 40.7 %all-reduce = (f32[768]{0:T(1024)}, f32[64]{0:T(128)}, f32[64]{0:T(128)}) all-reduce(f32[768]{0:T(1024)} %get-tuple-element.108, f32[64]{0:T(128)} %get-tuple-element.106, f32[64]{0:T(128)} %get-tuple-element.104), channel_id=1, replica_groups=mesh['batch'=8,'tok'=4] {'batch','tok'}, use_global_device_ids=true, to_apply=%region_20.21 | all-reduce | flops 896 | bytes 7168 | tf_op jit(solution)/shard_map/psum | solution.py:180
  729.0 9.9 %fusion.84 = bf16[768,768]{1,0:T(8,128)(2,1)} fusion(bf16[3,256,768]{2,1,0:T(8,128)(2,1)S(1)} %copy-done.6, bf16[3840,768]{1,0:T(8,128)(2,1)} %all-gather.5.cloned.1.call-done, bf16[768,3072]{1,0:T(8,128)(2,1)} %get-tuple-element.157, bf16[768,768]{1,0:T(8,128)(2,1)S(1)} %copy-done.18, f32[768]{0:T(1024)S(1)} %copy-done.27), kind=kOutput, calls=%fused_computation.107 | convolution fusion | flops 4544004096 | bytes 14158848 | tf_op jit(solution)/shard_map/dot_general | solution.py:116
  738.9 119.7 %reduce-scatter.3.cloned.1.call-done = f32[24,5376]{1,0:T(8,128)} async-done(((f32[768,5376]{1,0:T(8,128)}), f32[24,5376]{1,0:T(8,128)}) %reduce-scatter.3.cloned.1.call-update) | async-done | bytes 516112 | tf_op jit(solution)/shard_map/reduce_scatter | solution.py:173
  (276 shorter events, 368.0 us)
Async XLA Ops:
  7.2 74.2 %all-gather.5.cloned.1.call-start = ((), (), s32[]{:S(2)}) async-start(), calls=%async_computation.11 | async-start | bytes 6082560 | tf_op jit(solution)/shard_map/all_gather | solution.py:115
  7.9 153.7 %all-gather.3.cloned.1.call-start = ((), (), s32[]{:S(2)}) async-start(), calls=%async_computation.10 | async-start | bytes 8515584 | tf_op jit(solution)/shard_map/all_gather | solution.py:90
  11.8 77.1 %copy-start.19 = (bf16[768,768]{1,0:T(8,128)(2,1)}, bf16[768,768]{1,0:T(8,128)(2,1)S(1)}, u32[]{:S(2)}) copy-start(bf16[768,768]{1,0:T(8,128)(2,1)S(1)} %fusion.68) | copy-start | bytes 3538948
  100.5 61.2 %copy-start.15 = (bf16[768,768]{1,0:T(8,128)(2,1)S(1)}, bf16[768,768]{1,0:T(8,128)(2,1)}, u32[]{:S(2)}) copy-start(bf16[768,768]{1,0:T(8,128)(2,1)} %fusion.76) | copy-start | bytes 3538948
  100.5 90.8 %all-to-all-start.4 = ((bf16[3,256,12,64]{1,3,0,2:T(8,128)(2,1)}), bf16[3,256,12,64]{1,3,0,2:T(8,128)(2,1)}, u32[]{:S(2)}, u32[]{:S(2)}) async-start(bf16[3,256,12,64]{1,3,0,2:T(8,128)(2,1)} %copy.183), calls=%async_computation.4 | async-start | bytes 2359296 | tf_op jit(solution)/shard_map/all_to_all | solution.py:131
  191.3 30.8 %all-to-all-start = ((bf16[3,256,12,64]{1,3,0,2:T(8,128)(2,1)}), bf16[3,256,12,64]{1,3,0,2:T(8,128)(2,1)S(1)}, u32[]{:S(2)}, u32[]{:S(2)}) async-start(bf16[3,256,12,64]{1,3,0,2:T(8,128)(2,1)} %copy.166), calls=%async_computation | async-start | bytes 2359296 | tf_op jit(solution)/shard_map/all_to_all | solution.py:108
  222.1 20.2 %all-to-all-start.1 = ((bf16[3,256,12,64]{1,3,0,2:T(8,128)(2,1)}), bf16[3,256,12,64]{1,3,0,2:T(8,128)(2,1)}, u32[]{:S(2)}, u32[]{:S(2)}) async-start(bf16[3,256,12,64]{1,3,0,2:T(8,128)(2,1)} %copy.171), calls=%async_computation.1 | async-start | bytes 2359296 | tf_op jit(solution)/shard_map/all_to_all | solution.py:106
  236.1 9.8 %copy-start.32 = (s32[3,256]{1,0:T(4,128)S(1)}, s32[3,256]{1,0:T(4,128)}, u32[]{:S(2)}) copy-start(s32[3,256]{1,0:T(4,128)} %param.13) | copy-start | bytes 9220
  242.3 30.7 %all-to-all-start.2 = ((bf16[3,256,12,64]{1,3,0,2:T(8,128)(2,1)}), bf16[3,256,12,64]{1,3,0,2:T(8,128)(2,1)S(1)}, u32[]{:S(2)}, u32[]{:S(2)}) async-start(bf16[3,256,12,64]{1,3,0,2:T(8,128)(2,1)} %copy.176), calls=%async_computation.2 | async-start | bytes 2359296 | tf_op jit(solution)/shard_map/all_to_all | solution.py:107
  330.0 20.2 %all-to-all-start.3 = ((bf16[4,2,73728]{2,1,0:T(2,128)(2,1)}), bf16[4,2,73728]{2,1,0:T(2,128)(2,1)}, u32[]{:S(2)}, u32[]{:S(2)}) async-start(bf16[4,2,73728]{2,1,0:T(2,128)(2,1)} %reshape.419), calls=%async_computation.3 | async-start | bytes 2359296 | tf_op jit(solution)/shard_map/all_to_all | solution.py:113
  334.3 404.6 %reduce-scatter.5.cloned.1.call-start = ((), (), s32[]{:S(2)}) async-start(), calls=%async_computation.13 | async-start | bytes 12165120 | tf_op jit(solution)/shard_map/reduce_scatter | solution.py:166
  360.2 11.9 %copy-start.17 = (bf16[768,768]{1,0:T(8,128)(2,1)}, bf16[768,768]{1,0:T(8,128)(2,1)S(1)}, u32[]{:S(2)}) copy-start(bf16[768,768]{1,0:T(8,128)(2,1)S(1)} %copy.181) | copy-start | bytes 3538948
  467.5 30.2 %all-to-all-start.7 = ((bf16[4,2,73728]{2,1,0:T(2,128)(2,1)}), bf16[4,2,73728]{2,1,0:T(2,128)(2,1)}, u32[]{:S(2)}, u32[]{:S(2)}) async-start(bf16[4,2,73728]{2,1,0:T(2,128)(2,1)} %reshape.421), calls=%async_computation.7 | async-start | bytes 2359296 | tf_op jit(solution)/shard_map/all_to_all | solution.py:138
  497.7 23.1 %all-to-all-start.5 = ((bf16[4,2,73728]{2,1,0:T(2,128)(2,1)}), bf16[4,2,73728]{2,1,0:T(2,128)(2,1)}, u32[]{:S(2)}, u32[]{:S(2)}) async-start(bf16[4,2,73728]{2,1,0:T(2,128)(2,1)} %reshape.425), calls=%async_computation.5 | async-start | bytes 2359296 | tf_op jit(solution)/shard_map/all_to_all | solution.py:136
  506.9 18.3 %copy-start.36 = (f32[64]{0:T(128)S(1)}, f32[64]{0:T(128)}, u32[]{:S(2)}) copy-start(f32[64]{0:T(128)} %param.16) | copy-start | bytes 772
  506.9 18.4 %copy-start.38 = (f32[64]{0:T(128)S(1)}, f32[64]{0:T(128)}, u32[]{:S(2)}) copy-start(f32[64]{0:T(128)} %param.17) | copy-start | bytes 772
  520.8 87.8 %all-to-all-start.6 = ((bf16[4,2,73728]{2,1,0:T(2,128)(2,1)}), bf16[4,2,73728]{2,1,0:T(2,128)(2,1)}, u32[]{:S(2)}, u32[]{:S(2)}) async-start(bf16[4,2,73728]{2,1,0:T(2,128)(2,1)} %reshape.423), calls=%async_computation.6 | async-start | bytes 2359296 | tf_op jit(solution)/shard_map/all_to_all | solution.py:137
  525.1 333.5 %reduce-scatter.3.cloned.1.call-start = ((), (), s32[]{:S(2)}) async-start(), calls=%async_computation.12 | async-start | bytes 17031168 | tf_op jit(solution)/shard_map/reduce_scatter | solution.py:173
  525.3 7.9 copy-start.12
  525.3 7.9 copy-start.4
  645.8 10.5 %copy-start.16 = (bf16[768,768]{1,0:T(8,128)(2,1)S(1)}, bf16[768,768]{1,0:T(8,128)(2,1)}, u32[]{:S(2)}) copy-start(bf16[768,768]{1,0:T(8,128)(2,1)} %fusion.76) | copy-start | bytes 3538948
  645.8 10.5 %copy-start.21 = (bf16[768,768]{1,0:T(8,128)(2,1)S(1)}, bf16[768,768]{1,0:T(8,128)(2,1)}, u32[]{:S(2)}) copy-start(bf16[768,768]{1,0:T(8,128)(2,1)} %copy.218) | copy-start | bytes 3538948
  669.8 55.4 %copy-start.11 = (bf16[3,256,768]{2,1,0:T(8,128)(2,1)S(1)}, bf16[3,256,768]{2,1,0:T(8,128)(2,1)}, u32[]{:S(2)}) copy-start(bf16[3,256,768]{2,1,0:T(8,128)(2,1)} %param.14) | copy-start | bytes 3538948
  669.9 55.4 %copy-start.27 = (f32[768]{0:T(1024)S(1)}, f32[768]{0:T(1024)}, u32[]{:S(2)}) copy-start(f32[768]{0:T(1024)} %copy-done.26) | copy-start | bytes 9220
  (29 other events, 100.5 us)
Sparse Core Ops, SparseCore 0:
  10.9 70.3 all-gather.4
  84.3 77.3 all-gather.2
  372.3 156.6 reduce-scatter.4
  668.7 189.7 reduce-scatter.2
where the time goes:
time: 876 us; the launch traced here: 865 us
  waiting for transfers between devices  283 us (32%)
  local copies, waits for them, and re-layouts  218 us (25%)
  matrix products  151 us (17%)
  other arithmetic  94.8 us (11%)
  blocking collectives  57.5 us (7%)
  starting transfers between devices  45.3 us (5%)
  between operations  14.8 us (2%)
    reduce_scatter x1, waiting for transfers between devices, per_device(): lax.psum_scatter(lax.dot_general(columns, grad_merged, contract_first, pr...  120 us
    all_gather x1, waiting for transfers between devices, per_device(): out_full = lax.all_gather(out_weight, ('batch', 'tok'), axis=0, tiled=True)  68.2 us
    all_gather x1, waiting for transfers between devices, per_device(): in_full = lax.all_gather(in_weight, ('batch', 'tok'), axis=0, tiled=True)  56.8 us
    unnamed x94, local copies, waits for them, and re-layouts  42.2 us
    psum x1, blocking collectives, per_device(): lax.psum((norm_grad, query_grad, key_grad), ('batch', 'tok'))  40.7 us
    dot_general x3, matrix products, backward_sequence(): jnp.einsum('qhd,khd->hqk', grad_out, value_block, preferred_element_type=...  24.8 us
    another operation x2, other arithmetic  23.5 us
    convert_element_type x3, other arithmetic, backward_sequence(): grad_scores = (probabilities * (grad_probs - weighted)).astype(jnp.bfloat16)  21.5 us
  transfers between devices with their start and end apart: 12, of which 8 were waited for; matrix products, arithmetic and copies ran while one was open for 43% of the time, Pallas kernels for 0%

commit v1 on v0

--- a/solution.py
+++ b/solution.py
@@ -1,13 +1,24 @@
+import functools
 import math
 import jax
 import jax.numpy as jnp
 from jax import lax
 from jax.sharding import PartitionSpec as P
+from jax.lax import all_to_all, axis_size
 
 H = 12
 HD = 64
 mask_fill = -1000000000.0
 norm_eps = 1e-06
+
+
+def _draft_vectors(matrix, pos_dim, k_dim):
+    return jnp.concatenate(
+        all_to_all(jnp.stack(jnp.split(matrix, axis_size("tok"), pos_dim), 0), "tok", 0, 0), k_dim
+    )
+
+
+_recover_sizes = functools.partial(_draft_vectors, pos_dim=1, k_dim=2)
 
 
 def normalize(values):
@@ -133,7 +144,7 @@
         backward_sequence, (query_heads, key_heads, value_heads, ids_full, log_total, grad_heads_h)
     )
     grad_query, grad_key, grad_value = (
-        lax.all_to_all(grad_query_h, "tok", split_axis=1, concat_axis=2, tiled=True),
+        _recover_sizes(grad_query_h),
         lax.all_to_all(grad_key_h, "tok", split_axis=1, concat_axis=2, tiled=True),
         lax.all_to_all(grad_value_h, "tok", split_axis=1, concat_axis=2, tiled=True),
     )

time: 876 us -> 849 us (0.969)
  local copies, waits for them, and re-layouts: 218 us -> 198 us
  starting transfers between devices: 45.3 us -> 33.4 us
    all_to_all x1, starting transfers between devices: 15.2 us -> 3.99 us  [per_device(): lax.all_to_all(value_rows, 'tok', split_axis=2, concat_axis=1, tiled=True)]
    unnamed x94 -> x102, local copies, waits for them, and re-layouts: 42.2 us -> 35.8 us
    another operation x2 -> x3, other arithmetic: 23.5 us -> 24.7 us
  transfers between devices with their start and end apart: 12 -> 12, of which waited for: 8 -> 8; matrix products, arithmetic and copies ran while one was open for 43% -> 42% of each run, Pallas kernels for 0% -> 0%
where the time goes in v1:
time: 849 us; the launch traced here: 838 us
  waiting for transfers between devices  288 us (34%)
  local copies, waits for them, and re-layouts  198 us (23%)
  matrix products  151 us (18%)
  other arithmetic  95.6 us (11%)
  blocking collectives  57.6 us (7%)
  starting transfers between devices  33.4 us (4%)
  between operations  14.8 us (2%)
    reduce_scatter x1, waiting for transfers between devices, per_device(): lax.psum_scatter(lax.dot_general(columns, grad_merged, contract_first, pr...  119 us
    all_gather x1, waiting for transfers between devices, per_device(): out_full = lax.all_gather(out_weight, ('batch', 'tok'), axis=0, tiled=True)  68.2 us
    all_gather x1, waiting for transfers between devices, per_device(): in_full = lax.all_gather(in_weight, ('batch', 'tok'), axis=0, tiled=True)  56.6 us
    psum x1, blocking collectives, per_device(): lax.psum((norm_grad, query_grad, key_grad), ('batch', 'tok'))  40.8 us
    unnamed x102, local copies, waits for them, and re-layouts  35.8 us
    dot_general x3, matrix products, backward_sequence(): jnp.einsum('qhd,khd->hqk', grad_out, value_block, preferred_element_type=...  24.6 us
    all_to_all x1, waiting for transfers between devices, per_device(): lax.all_to_all(grad_value_h, 'tok', split_axis=1, concat_axis=2, tiled=True)  23.7 us
    another operation x2, other arithmetic  23.5 us
  transfers between devices with their start and end apart: 12, of which 8 were waited for; matrix products, arithmetic and copies ran while one was open for 42% of the time, Pallas kernels for 0%

profile of v1, /device:TPU:0, one launch (start us, length us, event | category | flops | bytes accessed | tf_op | source)
XLA Modules:
  0.0 838.2 jit_solution(3552095954925895543)
XLA Ops:
  13.2 68.2 %all-gather.5.cloned.1.call-done = bf16[3840,768]{1,0:T(8,128)(2,1)} async-done(((bf16[120,768]{1,0:T(8,128)(2,1)}), bf16[3840,768]{1,0:T(8,128)(2,1)}) %all-gather.5.cloned.1.call-update) | async-done | bytes 5898256 | tf_op jit(solution)/shard_map/all_gather | solution.py:126
  81.4 7.4 fusion.93
  105.1 56.6 %all-gather.3.cloned.1.call-done = bf16[768,5376]{1,0:T(8,128)(2,1)} async-done(((bf16[24,5376]{1,0:T(8,128)(2,1)}), bf16[768,5376]{1,0:T(8,128)(2,1)}) %all-gather.3.cloned.1.call-update) | async-done | bytes 8257552 | tf_op jit(solution)/shard_map/all_gather | solution.py:101
  161.7 8.7 %fusion.92 = f32[768,5376]{1,0:T(8,128)S(1)} fusion(bf16[768,768]{1,0:T(8,128)(2,1)S(1)} %copy-done.18, bf16[768,5376]{1,0:T(8,128)(2,1)} %all-gather.3.cloned.1.call-done), kind=kOutput, calls=%fused_computation.147 | convolution fusion | flops 6341787648 | bytes 25952256 | tf_op jit(solution)/shard_map/dot_general | solution.py:102
  234.7 16.8 %all_gather.12 = s32[3,1024]{1,0:T(4,128)S(1)} all-gather(s32[3,256]{1,0:T(4,128)S(1)} %copy-done.37), channel_id=1, replica_groups=mesh['batch'=8,'tok'=4] {'tok'}, dimensions={1}, use_global_device_ids=true | all-gather | bytes 15360 | tf_op jit(solution)/shard_map/all_gather | solution.py:115
  265.6 45.7 %while.26 = (s32[]{:T(128)}, bf16[3,1024,3,64]{1,3,2,0:T(8,128)(2,1)}, f32[3,3,1024]{2,1,0:T(4,128)}, bf16[3,1024,3,64]{1,3,2,0:T(8,128)(2,1)}, s32[3,1024]{1,0:...) while((s32[]{:T(128)}, ...), condition=%wide.region_9.10_spmd, body=%wide.region_6.9_spmd.sunk | while | flops 845346816 | bytes 47833216 | solution.py:121
  323.4 14.1 %fusion.65 = (bf16[768,3072]{1,0:T(8,128)(2,1)}, bf16[768,3072]{1,0:T(8,128)(2,1)}) fusion(f32[768,3840]{1,0:T(8,128)} %copy-done.7, f32[768,5376]{1,0:T(8,128)} %copy-done.1), kind=kLoop, calls=%fused_computation.76 | loop fusion | flops 51904512 | bytes 28311552 | tf_op jit(solution)/shard_map/convert.17
  349.1 11.8 %fusion.66 = f32[3840,768]{1,0:T(8,128)} fusion(bf16[768,768]{1,0:T(8,128)(2,1)S(1)} %copy-done.23, bf16[768,3072]{1,0:T(8,128)(2,1)} %get-tuple-element.157, bf16[768,768]{1,0:T(8,128)(2,1)S(1)} %copy.232), kind=kOutput, calls=%fused_computation.80 | convolution fusion | flops 4541644800 | bytes 18874368 | tf_op jit(solution)/shard_map/dot_general | solution.py:178
  364.6 83.9 %while.27 = (s32[]{:T(128)}, bf16[3,1024,3,64]{1,3,2,0:T(8,128)(2,1)}, bf16[3,1024,3,64]{1,3,2,0:T(8,128)(2,1)}, bf16[3,1024,3,64]{1,3,2,0:T(8,128)(2,1)}, bf16[...) while((s32[]{:T(128)}, ...), condition=%wide.region_12.13_spmd, body=%wide.region_10.12_spmd.sunk | while | flops 2063529984 | bytes 102616192 | solution.py:143
  368.1 8.2 multiply_reduce_fusion.11
  376.4 7.5 multiply_convert_fusion.7
  396.4 8.2 multiply_reduce_fusion.11
  424.0 8.2 multiply_reduce_fusion.11
  461.2 23.7 %all-to-all-done.7 = bf16[4,2,73728]{2,1,0:T(2,128)(2,1)S(1)} async-done(((bf16[4,2,73728]{2,1,0:T(2,128)(2,1)}), bf16[4,2,73728]{2,1,0:T(2,128)(2,1)S(1)}, u32[]{:S(2)}, u32[]{:S(2)}) %all-to-all-start.7) | async-done | bytes 1179680 | tf_op jit(solution)/shard_map/all_to_all | solution.py:149
  497.0 9.9 %all-to-all-done.5 = bf16[4,3,256,3,64]{2,4,3,1,0:T(8,128)(2,1)} async-done(((bf16[4,3,256,3,64]{2,4,3,1,0:T(8,128)(2,1)}), bf16[4,3,256,3,64]{2,4,3,1,0:T(8,128)(2,1)}, u32[]{:S(2)}, u32[]{:S(2)}) %all-to-all-start.5) | async-done | bytes 1179680 | tf_op jit(solution)/shard_map/all_to_all | solution.py:17
  511.8 7.8 reshape.409
  574.0 7.7 reshape.408
  611.2 7.8 reshape.410
  619.0 9.4 %multiply_convert_fusion.5 = (bf16[768,768]{1,0:T(8,128)(2,1)S(1)}, bf16[768,768]{1,0:T(8,128)(2,1)S(1)}) fusion(f32[768,768]{1,0:T(8,128)S(1)} %copy-done.8, f32[768,768]{1,0:T(8,128)} %copy.248, f32[768,768]{1,0:T(8,128)} %copy.241, f32[768,768]{1,0:T(8,128)} %copy.240, f32[768,768]{1,0:T(8,128)} %reshape.408, f32[768]{0:T(1024)S(1)} %mul.317, ...), kind=kLoop, calls=%fused_computation.114 | loop fusion | flops 9437184 | bytes 30676992 | tf_op jit(solution)/shard_map/convert.14
  629.4 12.1 %fusion.85 = f32[768,5376]{1,0:T(8,128)} fusion(bf16[768,768]{1,0:T(8,128)(2,1)S(1)} %copy-done.19, bf16[768,3072]{1,0:T(8,128)(2,1)} %get-tuple-element.156, bf16[768,768]{1,0:T(8,128)(2,1)S(1)} %copy-done.24, bf16[768,768]{1,0:T(8,128)(2,1)S(1)} %get-tuple-element.155, bf16[768,768]{1,0:T(8,128)(2,1)S(1)} %get-tuple-element.154), kind=kOutput, calls=%fused_computation.122 | convolution fusion | flops 6374817792 | bytes 25952256 | tf_op jit(solution)/shard_map/dot_general | solution.py:185
  642.8 13.4 %fusion.82 = (f32[768]{0:T(1024)}, f32[768]{0:T(1024)}, f32[768]{0:T(1024)}, f32[768,768]{1,0:T(8,128)}) fusion(bf16[3,256,768]{2,1,0:T(8,128)(2,1)S(1)} %copy-done.6, f32[768]{0:T(1024)S(1)} %copy-done.36, f32[768]{0:T(1024)S(1)} %copy-done.34, f32[768]{0:T(1024)S(1)} %copy-done.39, bf16[768,5376]{1,0:T(8,128)(2,1)} %all-gather.3.cloned.1.call-done, ...), kind=kOutput, calls=%fused_computation.105 | convolution fusion | flops 6380123136 | bytes 20072448 | tf_op jit(solution)/shard_map/dot_general | solution.py:173
  656.1 40.8 %all-reduce = (f32[768]{0:T(1024)}, f32[64]{0:T(128)}, f32[64]{0:T(128)}) all-reduce(f32[768]{0:T(1024)} %get-tuple-element.108, f32[64]{0:T(128)} %get-tuple-element.106, f32[64]{0:T(128)} %get-tuple-element.104), channel_id=1, replica_groups=mesh['batch'=8,'tok'=4] {'batch','tok'}, use_global_device_ids=true, to_apply=%region_20.21 | all-reduce | flops 896 | bytes 7168 | tf_op jit(solution)/shard_map/psum | solution.py:191
  702.1 9.9 %fusion.84 = bf16[768,768]{1,0:T(8,128)(2,1)} fusion(bf16[3,256,768]{2,1,0:T(8,128)(2,1)S(1)} %copy-done.6, bf16[3840,768]{1,0:T(8,128)(2,1)} %all-gather.5.cloned.1.call-done, bf16[768,3072]{1,0:T(8,128)(2,1)} %get-tuple-element.157, bf16[768,768]{1,0:T(8,128)(2,1)S(1)} %copy-done.21, f32[768]{0:T(1024)S(1)} %copy-done.32), kind=kOutput, calls=%fused_computation.107 | convolution fusion | flops 4544004096 | bytes 14158848 | tf_op jit(solution)/shard_map/dot_general | solution.py:127
  712.0 119.5 %reduce-scatter.3.cloned.1.call-done = f32[24,5376]{1,0:T(8,128)} async-done(((f32[768,5376]{1,0:T(8,128)}), f32[24,5376]{1,0:T(8,128)}) %reduce-scatter.3.cloned.1.call-update) | async-done | bytes 516112 | tf_op jit(solution)/shard_map/reduce_scatter | solution.py:184
  (280 shorter events, 345.4 us)
Async XLA Ops:
  7.2 74.2 %all-gather.5.cloned.1.call-start = ((), (), s32[]{:S(2)}) async-start(), calls=%async_computation.11 | async-start | bytes 6082560 | tf_op jit(solution)/shard_map/all_gather | solution.py:126
  7.9 153.7 %all-gather.3.cloned.1.call-start = ((), (), s32[]{:S(2)}) async-start(), calls=%async_computation.10 | async-start | bytes 8515584 | tf_op jit(solution)/shard_map/all_gather | solution.py:101
  11.8 77.1 %copy-start.22 = (bf16[768,768]{1,0:T(8,128)(2,1)}, bf16[768,768]{1,0:T(8,128)(2,1)S(1)}, u32[]{:S(2)}) copy-start(bf16[768,768]{1,0:T(8,128)(2,1)S(1)} %fusion.68) | copy-start | bytes 3538948
  100.7 61.0 %copy-start.18 = (bf16[768,768]{1,0:T(8,128)(2,1)S(1)}, bf16[768,768]{1,0:T(8,128)(2,1)}, u32[]{:S(2)}) copy-start(bf16[768,768]{1,0:T(8,128)(2,1)} %fusion.76) | copy-start | bytes 3538948
  100.7 90.5 %all-to-all-start.4 = ((bf16[3,256,12,64]{1,3,0,2:T(8,128)(2,1)}), bf16[3,256,12,64]{1,3,0,2:T(8,128)(2,1)}, u32[]{:S(2)}, u32[]{:S(2)}) async-start(bf16[3,256,12,64]{1,3,0,2:T(8,128)(2,1)} %copy.234), calls=%async_computation.4 | async-start | bytes 2359296 | tf_op jit(solution)/shard_map/all_to_all | solution.py:142
  191.2 19.8 %all-to-all-start = ((bf16[3,256,12,64]{1,3,0,2:T(8,128)(2,1)}), bf16[3,256,12,64]{1,3,0,2:T(8,128)(2,1)S(1)}, u32[]{:S(2)}, u32[]{:S(2)}) async-start(bf16[3,256,12,64]{1,3,0,2:T(8,128)(2,1)} %copy.217), calls=%async_computation | async-start | bytes 2359296 | tf_op jit(solution)/shard_map/all_to_all | solution.py:119
  211.0 20.2 %all-to-all-start.1 = ((bf16[3,256,12,64]{1,3,0,2:T(8,128)(2,1)}), bf16[3,256,12,64]{1,3,0,2:T(8,128)(2,1)}, u32[]{:S(2)}, u32[]{:S(2)}) async-start(bf16[3,256,12,64]{1,3,0,2:T(8,128)(2,1)} %copy.222), calls=%async_computation.1 | async-start | bytes 2359296 | tf_op jit(solution)/shard_map/all_to_all | solution.py:117
  225.0 9.7 %copy-start.37 = (s32[3,256]{1,0:T(4,128)S(1)}, s32[3,256]{1,0:T(4,128)}, u32[]{:S(2)}) copy-start(s32[3,256]{1,0:T(4,128)} %param.13) | copy-start | bytes 9220
  231.2 30.7 %all-to-all-start.2 = ((bf16[3,256,12,64]{1,3,0,2:T(8,128)(2,1)}), bf16[3,256,12,64]{1,3,0,2:T(8,128)(2,1)S(1)}, u32[]{:S(2)}, u32[]{:S(2)}) async-start(bf16[3,256,12,64]{1,3,0,2:T(8,128)(2,1)} %copy.227), calls=%async_computation.2 | async-start | bytes 2359296 | tf_op jit(solution)/shard_map/all_to_all | solution.py:118
  318.9 20.2 %all-to-all-start.3 = ((bf16[4,2,73728]{2,1,0:T(2,128)(2,1)}), bf16[4,2,73728]{2,1,0:T(2,128)(2,1)}, u32[]{:S(2)}, u32[]{:S(2)}) async-start(bf16[4,2,73728]{2,1,0:T(2,128)(2,1)} %reshape.412), calls=%async_computation.3 | async-start | bytes 2359296 | tf_op jit(solution)/shard_map/all_to_all | solution.py:124
  323.2 388.8 %reduce-scatter.5.cloned.1.call-start = ((), (), s32[]{:S(2)}) async-start(), calls=%async_computation.13 | async-start | bytes 12165120 | tf_op jit(solution)/shard_map/reduce_scatter | solution.py:177
  349.1 11.8 %copy-start.20 = (bf16[768,768]{1,0:T(8,128)(2,1)}, bf16[768,768]{1,0:T(8,128)(2,1)S(1)}, u32[]{:S(2)}) copy-start(bf16[768,768]{1,0:T(8,128)(2,1)S(1)} %copy.232) | copy-start | bytes 3538948
  456.2 28.8 %all-to-all-start.7 = ((bf16[4,2,73728]{2,1,0:T(2,128)(2,1)}), bf16[4,2,73728]{2,1,0:T(2,128)(2,1)S(1)}, u32[]{:S(2)}, u32[]{:S(2)}) async-start(bf16[4,2,73728]{2,1,0:T(2,128)(2,1)} %reshape.414), calls=%async_computation.7 | async-start | bytes 2359296 | tf_op jit(solution)/shard_map/all_to_all | solution.py:149
  485.0 21.9 %all-to-all-start.5 = ((bf16[4,3,256,3,64]{2,4,3,1,0:T(8,128)(2,1)}), bf16[4,3,256,3,64]{2,4,3,1,0:T(8,128)(2,1)}, u32[]{:S(2)}, u32[]{:S(2)}) async-start(bf16[4,3,256,3,64]{2,4,3,1,0:T(8,128)(2,1)} %pad_maximum_fusion.8), calls=%async_computation.5 | async-start | bytes 2359296 | tf_op jit(solution)/shard_map/all_to_all | solution.py:17
  493.9 17.7 %copy-start.41 = (f32[64]{0:T(128)S(1)}, f32[64]{0:T(128)}, u32[]{:S(2)}) copy-start(f32[64]{0:T(128)} %param.16) | copy-start | bytes 772
  493.9 17.8 %copy-start.43 = (f32[64]{0:T(128)S(1)}, f32[64]{0:T(128)}, u32[]{:S(2)}) copy-start(f32[64]{0:T(128)} %param.17) | copy-start | bytes 772
  506.9 74.9 %all-to-all-start.6 = ((bf16[4,2,73728]{2,1,0:T(2,128)(2,1)}), bf16[4,2,73728]{2,1,0:T(2,128)(2,1)}, u32[]{:S(2)}, u32[]{:S(2)}) async-start(bf16[4,2,73728]{2,1,0:T(2,128)(2,1)} %reshape.416), calls=%async_computation.6 | async-start | bytes 2359296 | tf_op jit(solution)/shard_map/all_to_all | solution.py:148
  511.6 319.9 %reduce-scatter.3.cloned.1.call-start = ((), (), s32[]{:S(2)}) async-start(), calls=%async_computation.12 | async-start | bytes 17031168 | tf_op jit(solution)/shard_map/reduce_scatter | solution.py:184
  511.8 7.9 copy-start.15
  511.8 7.9 copy-start.4
  619.0 10.5 %copy-start.19 = (bf16[768,768]{1,0:T(8,128)(2,1)S(1)}, bf16[768,768]{1,0:T(8,128)(2,1)}, u32[]{:S(2)}) copy-start(bf16[768,768]{1,0:T(8,128)(2,1)} %fusion.76) | copy-start | bytes 3538948
  619.0 10.5 %copy-start.24 = (bf16[768,768]{1,0:T(8,128)(2,1)S(1)}, bf16[768,768]{1,0:T(8,128)(2,1)}, u32[]{:S(2)}) copy-start(bf16[768,768]{1,0:T(8,128)(2,1)} %copy.267) | copy-start | bytes 3538948
  642.8 55.6 %copy-start.13 = (bf16[3,256,768]{2,1,0:T(8,128)(2,1)S(1)}, bf16[3,256,768]{2,1,0:T(8,128)(2,1)}, u32[]{:S(2)}) copy-start(bf16[3,256,768]{2,1,0:T(8,128)(2,1)} %param.14) | copy-start | bytes 3538948
  642.8 55.5 %copy-start.32 = (f32[768]{0:T(1024)S(1)}, f32[768]{0:T(1024)}, u32[]{:S(2)}) copy-start(f32[768]{0:T(1024)} %copy-done.31) | copy-start | bytes 9220
  (34 other events, 117.6 us)
Sparse Core Ops, SparseCore 0:
  10.9 70.3 all-gather.4
  84.3 77.3 all-gather.2
  361.1 155.1 reduce-scatter.4
  641.7 189.7 reduce-scatter.2
